TPU v7x, 32 devices: a whole 2x2x4 slice. The times are simulated.
32 devices in a mesh: rep: 8 (over z, y), fsdp: 4 (over x, core).
Axes of the slice: x: 2, y: 2, z: 4, core: 2. Of those that a mesh axis runs over, the one named last changes fastest.
Arguments:
- tokens: bfloat16 [4096, 576], P(('rep', 'fsdp')), may hold values from -6 to 6
- positions: int32 [4096], P(('rep', 'fsdp')), may hold values from 0 to 1212, as said below
- seq_count: int32 [32], P(('rep', 'fsdp')), may hold values from 0 to 2, as said below
- w_query: bfloat16 [1, 576, 576], P(None, 'fsdp'), may hold values from -0.25 to 0.25
- w_keyval: bfloat16 [1, 576, 384], P(None, 'fsdp'), may hold values from -0.25 to 0.25
- w_out: bfloat16 [1, 576, 576], P(None, 'fsdp'), may hold values from -0.75 to 0.75
- w_gateup: bfloat16 [1, 576, 3072], P(None, 'fsdp'), may hold values from -0.25 to 0.25
- w_down: bfloat16 [1, 1536, 576], P(None, 'fsdp'), may hold values from -0.15625 to 0.15625
- gain_attn: bfloat16 [1, 576], P(None, 'fsdp'), may hold values from 0.099609375 to 1.8984375
- gain_mlp: bfloat16 [1, 576], P(None, 'fsdp'), may hold values from 0.099609375 to 1.8984375
- out_grad: bfloat16 [4096, 576], P(('rep', 'fsdp')), may hold values from -6 to 6
Outputs:
- out_act: float32 [4096, 576], P(('rep', 'fsdp'))
- in_grad: float32 [4096, 576], P(('rep', 'fsdp'))
- grad_query: float32 [1, 576, 576], P(None, 'fsdp')
- grad_keyval: float32 [1, 576, 384], P(None, 'fsdp')
- grad_out: float32 [1, 576, 576], P(None, 'fsdp')
- grad_gateup: float32 [1, 576, 3072], P(None, 'fsdp')
- grad_down: float32 [1, 1536, 576], P(None, 'fsdp')
- grad_gain_attn: float32 [1, 576], P(None, 'fsdp')
- grad_gain_mlp: float32 [1, 576], P(None, 'fsdp')
Inputs may be any that keep to these rules, and one draw needn't show every extreme that they name: Device d (rep index times 4 plus fsdp index) holds live sequences in its first seq_count[d] slots; the others hold data that no output may use. Some device fills all 2 slots. Within a sequence the positions rise by 1 to 3 from one token to the next; some sequence reaches the most.
All inputs are finite; a program needn't handle non-finite values.
Results may differ from a plain program's by a relative error of at most 0.015.
Values may be sent and summed in bfloat16 or wider, within the bound.
No kernel may reach another device: no remote copies, remote signals or barrier semaphores. Data moves between devices by JAX's collectives and lax.ppermute only.
A program may use at most 128 MiB of HBM per device.

v0:
```python
import jax
import jax.numpy as jnp
from jax import lax
from jax.sharding import PartitionSpec as P

HEADS = 9
KVH = 3
HD = 64
LAYERS = 1
LEN = 64
norm_eps = 1e-05
rope_base = 100000.0


def shortened(value):

    def short(part):
        return part.astype(jnp.bfloat16) if part.dtype == jnp.float32 else part

    return jax.tree.map(short, value)


def inverse_rms(stream):
    return lax.rsqrt(jnp.mean(stream * stream, axis=-1, keepdims=True) + norm_eps)


def rope_tables(positions):
    half_size = HD // 2
    frequency = rope_base ** (-(jnp.arange(half_size, dtype=jnp.float32) * 2.0 / HD))
    angle_table = positions.astype(jnp.float32)[:, None] * frequency[None, :]
    angle_table = jnp.concatenate([angle_table, angle_table], axis=-1)[:, None, :]
    return (jnp.cos(angle_table), jnp.sin(angle_table))


def rotate(values, cosine, sine_table):
    half_size = values.shape[-1] // 2
    turned = jnp.concatenate([-values[..., half_size:], values[..., :half_size]], axis=-1)
    return values * cosine + turned * sine_table


def rotate_back(grad_rot, cosine, sine_table):
    half_size = grad_rot.shape[-1] // 2
    scaled = grad_rot * sine_table
    turned = jnp.concatenate([scaled[..., half_size:], -scaled[..., :half_size]], axis=-1)
    return grad_rot * cosine + turned


def masked_scores(query_rot, key_rot, causal):
    scores = jnp.einsum(
        "sqkgd,spkd->skgqp", query_rot, key_rot, preferred_element_type=jnp.float32
    ) * HD ** (-0.5)
    return jnp.where(causal, scores, -1e30)


def forward_layer(stream, weights, cosine, sine_table, causal, seq_total):
    w_query, w_keyval, w_out, w_gateup, w_down, gain_attn, gain_mlp = weights
    row_count = stream.shape[0]
    seq_len = row_count // seq_total
    kv_width = KVH * HD
    inv_attn = inverse_rms(stream)
    normed = (stream * inv_attn * gain_attn.astype(jnp.float32)).astype(jnp.bfloat16)
    query_raw = jnp.dot(normed, w_query, preferred_element_type=jnp.float32)
    keyval = jnp.dot(normed, w_keyval, preferred_element_type=jnp.float32)
    query_rot = rotate(query_raw.reshape(row_count, HEADS, HD), cosine, sine_table).astype(
        jnp.bfloat16
    )
    query_rot = query_rot.reshape(seq_total, seq_len, KVH, HEADS // KVH, HD)
    key_rot = rotate(keyval[:, :kv_width].reshape(row_count, KVH, HD), cosine, sine_table).astype(
        jnp.bfloat16
    )
    key_rot = key_rot.reshape(seq_total, seq_len, KVH, HD)
    value_part = keyval[:, kv_width:].astype(jnp.bfloat16).reshape(seq_total, seq_len, KVH, HD)
    scores = masked_scores(query_rot, key_rot, causal)
    row_peak = jnp.max(scores, axis=-1, keepdims=True)
    exponent = jnp.exp(scores - row_peak)
    row_total = jnp.sum(exponent, axis=-1, keepdims=True)
    probs = (exponent / row_total).astype(jnp.bfloat16)
    log_total = row_peak + jnp.log(row_total)
    mixed_out = jnp.einsum(
        "skgqp,spkd->sqkgd", probs, value_part, preferred_element_type=jnp.float32
    )
    mixed_out = mixed_out.reshape(row_count, HEADS * HD).astype(jnp.bfloat16)
    stream_mid = stream + jnp.dot(mixed_out, w_out, preferred_element_type=jnp.float32)
    inv_mlp = inverse_rms(stream_mid)
    normed_mid = (stream_mid * inv_mlp * gain_mlp.astype(jnp.float32)).astype(jnp.bfloat16)
    gateup = jnp.dot(normed_mid, w_gateup, preferred_element_type=jnp.float32)
    ff_width = gateup.shape[1] // 2
    hidden = (jax.nn.silu(gateup[:, :ff_width]) * gateup[:, ff_width:]).astype(jnp.bfloat16)
    result = stream_mid + jnp.dot(hidden, w_down, preferred_element_type=jnp.float32)
    kept = (
        stream,
        inv_attn,
        normed,
        query_rot,
        key_rot,
        value_part,
        log_total,
        mixed_out,
        stream_mid,
        inv_mlp,
        normed_mid,
        gateup,
        hidden,
    )
    return (result, kept)


def backward_mlp(d_stream, kept, weights):
    (
        stream,
        inv_attn,
        normed,
        query_rot,
        key_rot,
        value_part,
        log_total,
        mixed_out,
        stream_mid,
        inv_mlp,
        normed_mid,
        gateup,
        hidden,
    ) = kept
    w_query, w_keyval, w_out, w_gateup, w_down, gain_attn, gain_mlp = weights
    ff_width = gateup.shape[1] // 2
    d_branch = d_stream.astype(jnp.bfloat16)
    grad_down = jnp.einsum("nf,nd->fd", hidden, d_branch, preferred_element_type=jnp.float32)
    d_hidden = jnp.einsum("nd,fd->nf", d_branch, w_down, preferred_element_type=jnp.float32)
    gate_part = gateup[:, :ff_width]
    up_part = gateup[:, ff_width:]
    sigmoid_gate = jax.nn.sigmoid(gate_part)
    d_gate = d_hidden * up_part * sigmoid_gate * (1.0 + gate_part * (1.0 - sigmoid_gate))
    d_up = d_hidden * gate_part * sigmoid_gate
    d_gateup = jnp.concatenate([d_gate, d_up], axis=1).astype(jnp.bfloat16)
    grad_gateup = jnp.einsum("nd,nf->df", normed_mid, d_gateup, preferred_element_type=jnp.float32)
    d_normed_mid = jnp.einsum("nf,df->nd", d_gateup, w_gateup, preferred_element_type=jnp.float32)
    grad_gain_mlp = jnp.sum(d_normed_mid * stream_mid * inv_mlp, axis=0)
    scaled_mid = d_normed_mid * gain_mlp.astype(jnp.float32)
    d_mid = (
        d_stream
        + inv_mlp * scaled_mid
        - inv_mlp**3 * stream_mid * jnp.mean(scaled_mid * stream_mid, axis=-1, keepdims=True)
    )
    return (d_mid, (grad_gateup, grad_down, grad_gain_mlp))


def backward_attn(d_mid, kept, weights, cosine, sine_table, causal):
    (
        stream,
        inv_attn,
        normed,
        query_rot,
        key_rot,
        value_part,
        log_total,
        mixed_out,
        stream_mid,
        inv_mlp,
        normed_mid,
        gateup,
        hidden,
    ) = kept
    w_query, w_keyval, w_out, w_gateup, w_down, gain_attn, gain_mlp = weights
    row_count = stream.shape[0]
    d_attn = d_mid.astype(jnp.bfloat16)
    grad_out = jnp.einsum("nd,ne->de", mixed_out, d_attn, preferred_element_type=jnp.float32)
    d_mixed = jnp.einsum("ne,de->nd", d_attn, w_out, preferred_element_type=jnp.float32).astype(
        jnp.bfloat16
    )
    d_mixed = d_mixed.reshape(query_rot.shape)
    soft = jnp.exp(masked_scores(query_rot, key_rot, causal) - log_total)
    probs = soft.astype(jnp.bfloat16)
    d_value = jnp.einsum("skgqp,sqkgd->spkd", probs, d_mixed, preferred_element_type=jnp.float32)
    d_probs = jnp.einsum(
        "sqkgd,spkd->skgqp", d_mixed, value_part, preferred_element_type=jnp.float32
    )
    d_scores = (soft * (d_probs - jnp.sum(d_probs * soft, axis=-1, keepdims=True))).astype(
        jnp.bfloat16
    )
    d_query_rot = jnp.einsum(
        "skgqp,spkd->sqkgd", d_scores, key_rot, preferred_element_type=jnp.float32
    ) * HD ** (-0.5)
    d_key_rot = jnp.einsum(
        "skgqp,sqkgd->spkd", d_scores, query_rot, preferred_element_type=jnp.float32
    ) * HD ** (-0.5)
    d_query = rotate_back(d_query_rot.reshape(row_count, HEADS, HD), cosine, sine_table)
    d_query = d_query.reshape(row_count, HEADS * HD).astype(jnp.bfloat16)
    d_key = rotate_back(d_key_rot.reshape(row_count, KVH, HD), cosine, sine_table).reshape(
        row_count, KVH * HD
    )
    d_keyval = jnp.concatenate([d_key, d_value.reshape(row_count, KVH * HD)], axis=1).astype(
        jnp.bfloat16
    )
    grad_query = jnp.einsum("nd,ne->de", normed, d_query, preferred_element_type=jnp.float32)
    grad_keyval = jnp.einsum("nd,ne->de", normed, d_keyval, preferred_element_type=jnp.float32)
    d_normed = jnp.einsum("ne,de->nd", d_query, w_query, preferred_element_type=jnp.float32)
    d_normed = d_normed + jnp.einsum(
        "ne,de->nd", d_keyval, w_keyval, preferred_element_type=jnp.float32
    )
    grad_gain_attn = jnp.sum(d_normed * stream * inv_attn, axis=0)
    scaled_in = d_normed * gain_attn.astype(jnp.float32)
    d_input = (
        d_mid
        + inv_attn * scaled_in
        - inv_attn**3 * stream * jnp.mean(scaled_in * stream, axis=-1, keepdims=True)
    )
    return (d_input, (grad_query, grad_keyval, grad_out, grad_gain_attn))


def on_device(
    tokens,
    positions,
    seq_count,
    w_query,
    w_keyval,
    w_out,
    w_gateup,
    w_down,
    gain_attn,
    gain_mlp,
    out_grad,
):
    row_count = tokens.shape[0]
    seq_total = row_count // LEN
    live_seqs = (jnp.arange(seq_total, dtype=jnp.int32) < seq_count[0]).astype(jnp.float32)
    live_rows = jnp.repeat(live_seqs, LEN)[:, None]
    gathered = (
        lax.all_gather(w_query, "fsdp", axis=1, tiled=True),
        lax.all_gather(w_keyval, "fsdp", axis=1, tiled=True),
        lax.all_gather(w_out, "fsdp", axis=1, tiled=True),
        lax.all_gather(w_gateup, "fsdp", axis=1, tiled=True),
        lax.all_gather(w_down, "fsdp", axis=1, tiled=True),
        lax.all_gather(gain_attn, "fsdp", axis=1, tiled=True),
        lax.all_gather(gain_mlp, "fsdp", axis=1, tiled=True),
    )
    cosine, sine_table = rope_tables(positions)
    causal = jnp.arange(LEN)[:, None] >= jnp.arange(LEN)[None, :]
    stream = tokens.astype(jnp.float32)
    layer_index = 0
    layer_weights = tuple((weight[layer_index] for weight in gathered))
    stream, kept = forward_layer(stream, layer_weights, cosine, sine_table, causal, seq_total)
    kept_list = [kept]
    out_act = stream * live_rows
    gathered = (
        lax.all_gather(w_query, "fsdp", axis=1, tiled=True),
        lax.all_gather(w_keyval, "fsdp", axis=1, tiled=True),
        lax.all_gather(w_out, "fsdp", axis=1, tiled=True),
        lax.all_gather(w_gateup, "fsdp", axis=1, tiled=True),
        lax.all_gather(w_down, "fsdp", axis=1, tiled=True),
        lax.all_gather(gain_attn, "fsdp", axis=1, tiled=True),
        lax.all_gather(gain_mlp, "fsdp", axis=1, tiled=True),
    )
    d_stream = out_grad.astype(jnp.float32) * live_rows
    grad_list = [None] * LAYERS
    for layer_index in reversed(range(LAYERS)):
        layer_weights = tuple((weight[layer_index] for weight in gathered))
        d_mid, mlp_grads = backward_mlp(d_stream, kept_list[layer_index], layer_weights)
        d_stream, attn_grads = backward_attn(
            d_mid, kept_list[layer_index], layer_weights, cosine, sine_table, causal
        )
        grad_list[layer_index] = (
            attn_grads[0],
            attn_grads[1],
            attn_grads[2],
            mlp_grads[0],
            mlp_grads[1],
            attn_grads[3],
            mlp_grads[2],
        )
    stacked = tuple((jnp.stack([entry[member] for entry in grad_list]) for member in range(7)))
    shared = jax.tree.map(
        lambda part: part.astype(jnp.float32),
        lax.psum_scatter(shortened(stacked), "fsdp", scatter_dimension=1, tiled=True),
    )
    stacked = lax.psum(shared, "rep")
    return (out_act, d_stream) + tuple(stacked)


def solution(mesh):
    placed = (
        P(("rep", "fsdp"), None),
        P(("rep", "fsdp")),
        P(("rep", "fsdp")),
        P(None, "fsdp", None),
        P(None, "fsdp", None),
        P(None, "fsdp", None),
        P(None, "fsdp", None),
        P(None, "fsdp", None),
        P(None, "fsdp"),
        P(None, "fsdp"),
        P(("rep", "fsdp"), None),
    )
    return jax.shard_map(
        on_device,
        mesh=mesh,
        in_specs=placed,
        out_specs=(
            P(("rep", "fsdp"), None),
            P(("rep", "fsdp"), None),
            P(None, "fsdp", None),
            P(None, "fsdp", None),
            P(None, "fsdp", None),
            P(None, "fsdp", None),
            P(None, "fsdp", None),
            P(None, "fsdp"),
            P(None, "fsdp"),
        ),
        check_vma=False,
    )
```

profile of v0, /device:TPU:0, one launch (start us, length us, event | category | flops | bytes accessed | tf_op | source)
XLA Modules:
  0.0 433.5 jit_solution(7675057205242785737)
XLA Ops:
  11.5 1.0 fusion.37
  13.0 1.2 dynamic-slice
  15.3 8.3 %all-reduce.3 = (bf16[576]{0:T(1024)(128)(2,1)S(1)}, bf16[576]{0:T(1024)(128)(2,1)S(1)}) all-reduce(bf16[576]{0:T(1024)(128)(2,1)S(1)} %dynamic-update-slice, bf16[576]{0:T(1024)(128)(2,1)S(1)} %dynamic-update-slice.1), channel_id=1, replica_groups=mesh['rep'=8,'fsdp'=4] {'fsdp'}, use_global_device_ids=true, to_apply=%add | all-reduce | flops 1152 | bytes 4608
  23.8 9.4 %all_gather.29 = bf16[1,576,384]{2,1,0:T(8,128)(2,1)S(1)} all-gather(bf16[1,144,384]{2,1,0:T(8,128)(2,1)} %param.15), channel_id=1, replica_groups=mesh['rep'=8,'fsdp'=4] {'fsdp'}, dimensions={1}, use_global_device_ids=true | all-gather | bytes 552960 | tf_op jit(solution)/shard_map/all_gather | solution.py:229
  33.8 12.8 %all_gather.30 = bf16[1,576,576]{2,1,0:T(8,128)(2,1)S(1)} all-gather(bf16[1,144,576]{2,1,0:T(8,128)(2,1)S(1)} %copy-done.23), channel_id=1, replica_groups=mesh['rep'=8,'fsdp'=4] {'fsdp'}, dimensions={1}, use_global_device_ids=true | all-gather | bytes 829440 | tf_op jit(solution)/shard_map/all_gather | solution.py:228
  49.4 1.1 fusion.67
  52.1 8.7 %all_gather.31 = bf16[1,576,576]{2,1,0:T(8,128)(2,1)S(1)} all-gather(bf16[1,144,576]{2,1,0:T(8,128)(2,1)} %param.16), channel_id=1, replica_groups=mesh['rep'=8,'fsdp'=4] {'fsdp'}, dimensions={1}, use_global_device_ids=true | all-gather | bytes 829440 | tf_op jit(solution)/shard_map/all_gather | solution.py:230
  62.4 4.1 fusion.3
  66.5 5.3 %all-gather.5.cloned.1.call-done = bf16[1,1536,576]{1,2,0:T(8,128)(2,1)} async-done(((bf16[1,384,576]{1,2,0:T(8,128)(2,1)}), bf16[1,1536,576]{1,2,0:T(8,128)(2,1)}) %all-gather.5.cloned.1.call-update) | async-done | bytes 1769488 | tf_op jit(solution)/shard_map/all_gather | solution.py:232
  71.8 3.6 multiply_convert_fusion.1
  75.5 1.8 multiply_reduce_fusion.1
  77.4 1.0 convolution_convert_fusion.6
  78.5 1.1 reshape.234
  79.5 1.6 fusion.26
  81.1 1.1 multiply_reduce_fusion
  88.5 1.1 fusion.15
  89.6 1.2 fusion.11
  91.4 1.3 fusion.10
  93.3 6.0 %copy.98 = bf16[1,1536,576]{2,0,1:T(2,128)(2,1)} copy(bf16[1,1536,576]{1,2,0:T(8,128)(2,1)S(1)} %fusion.5) | data formatting | bytes 3538944
  99.3 3.8 copy.124
  103.2 0.9 copy-done.19
  104.2 2.9 fusion
  107.7 0.9 fusion.41
  108.6 1.3 fusion.20
  110.8 16.5 %reduce-scatter.24.cloned.1.call-done = bf16[144,1]{1,0:T(8,128)(2,1)} async-done(((bf16[576,1]{1,0:T(8,128)(2,1)}), bf16[144,1]{1,0:T(8,128)(2,1)}) %reduce-scatter.24.cloned.1.call-update) | async-done | bytes 304
  128.1 22.7 %reduce-scatter.16.cloned.1.call-done = bf16[1,144,384]{2,1,0:T(8,128)(2,1)} async-done(((bf16[1,576,384]{2,1,0:T(8,128)(2,1)}), bf16[1,144,384]{2,1,0:T(8,128)(2,1)}) %reduce-scatter.16.cloned.1.call-update) | async-done | bytes 110608 | tf_op jit(solution)/shard_map/reduce_scatter | solution.py:273
  150.8 26.0 %reduce-scatter.18.cloned.1.call-done = bf16[1,144,576]{2,1,0:T(8,128)(2,1)} async-done(((bf16[1,576,576]{2,1,0:T(8,128)(2,1)}), bf16[1,144,576]{2,1,0:T(8,128)(2,1)}) %reduce-scatter.18.cloned.1.call-update) | async-done | bytes 165904 | tf_op jit(solution)/shard_map/reduce_scatter | solution.py:273
  176.8 26.3 %reduce-scatter.14.cloned.1.call-done = bf16[1,144,576]{2,1,0:T(8,128)(2,1)} async-done(((bf16[1,576,576]{2,1,0:T(8,128)(2,1)}), bf16[1,144,576]{2,1,0:T(8,128)(2,1)}) %reduce-scatter.14.cloned.1.call-update) | async-done | bytes 165904 | tf_op jit(solution)/shard_map/reduce_scatter | solution.py:273
  203.1 33.2 %reduce-scatter.22.cloned.1.call-done = bf16[384,576]{1,0:T(8,128)(2,1)} async-done(((bf16[1536,576]{1,0:T(8,128)(2,1)}), bf16[384,576]{1,0:T(8,128)(2,1)}) %reduce-scatter.22.cloned.1.call-update) | async-done | bytes 442384
  236.3 1.5 reshape_bitcast_fusion
  238.5 41.0 %reduce-scatter.20.cloned.1.call-done = bf16[1,144,3072]{2,1,0:T(8,128)(2,1)} async-done(((bf16[1,576,3072]{2,1,0:T(8,128)(2,1)}), bf16[1,144,3072]{2,1,0:T(8,128)(2,1)}) %reduce-scatter.20.cloned.1.call-update) | async-done | bytes 884752 | tf_op jit(solution)/shard_map/reduce_scatter | solution.py:273
  279.5 147.5 %all-reduce.5 = (f32[1,144,576]{2,1,0:T(8,128)}, f32[1,144,384]{2,1,0:T(8,128)}, f32[1,144,576]{2,1,0:T(8,128)}, f32[1,144,3072]{2,1,0:T(8,128)}, f32[1,384,576]...) all-reduce(bf16[1,144,576]{2,1,0:T(8,128)(2,1)S(1)} %copy-done.25, ...), channel_id=1, replica_groups=mesh['rep'=8,'fsdp'=4] {'rep'}, use_global_device_ids=true, to_apply=%region_8.9 | all-reduce | flops 885024 | bytes 5310144 | tf_op jit(solution)/shard_map/psum | solution.py:275
  (157 shorter events, 21.6 us)
Async XLA Ops:
  7.2 26.0 %copy-start = (bf16[128,576]{0,1:T(8,128)(2,1)S(1)}, bf16[128,576]{0,1:T(8,128)(2,1)}, u32[]{:S(2)}) copy-start(bf16[128,576]{0,1:T(8,128)(2,1)} %param.11) | copy-start | bytes 442372
  7.2 26.6 %copy-start.23 = (bf16[1,144,576]{2,1,0:T(8,128)(2,1)S(1)}, bf16[1,144,576]{2,1,0:T(8,128)(2,1)}, u32[]{:S(2)}) copy-start(bf16[1,144,576]{2,1,0:T(8,128)(2,1)} %param.14) | copy-start | bytes 497668
  7.2 55.2 %all-gather.3.cloned.1.call-start = ((), (), s32[]{:S(2)}) async-start(), calls=%async_computation.7 | async-start | bytes 4423680 | tf_op jit(solution)/shard_map/all_gather | solution.py:231
  7.9 63.9 %all-gather.5.cloned.1.call-start = ((), (), s32[]{:S(2)}) async-start(), calls=%async_computation.8 | async-start | bytes 2211840 | tf_op jit(solution)/shard_map/all_gather | solution.py:232
  8.7 101.3 %reduce-scatter.26.cloned.1.call-start = ((), (), s32[]{:S(2)}) async-start(), calls=%async_computation.15 | async-start | bytes 184320
  23.8 23.6 %copy-start.8 = (f32[128,64]{0,1:T(8,128)}, f32[128,64]{0,1:T(8,128)S(1)}, u32[]{:S(2)}) copy-start(f32[128,64]{0,1:T(8,128)S(1)} %get-tuple-element.37) | copy-start | bytes 98308
  23.8 23.6 %copy-start.13 = (f32[128,64]{0,1:T(8,128)}, f32[128,64]{0,1:T(8,128)S(1)}, u32[]{:S(2)}) copy-start(f32[128,64]{0,1:T(8,128)S(1)} %get-tuple-element.38) | copy-start | bytes 98308
  48.9 2.7 copy-start.15
  52.1 14.4 %copy-start.4 = (bf16[128,576]{0,1:T(8,128)(2,1)}, bf16[128,576]{0,1:T(8,128)(2,1)S(1)}, u32[]{:S(2)}) copy-start(bf16[128,576]{0,1:T(8,128)(2,1)S(1)} %convert_element_type.167) | copy-start | bytes 442372
  62.4 9.4 %copy-start.10 = (bf16[128,576]{0,1:T(8,128)(2,1)S(1)}, bf16[128,576]{0,1:T(8,128)(2,1)}, u32[]{:S(2)}) copy-start(bf16[128,576]{0,1:T(8,128)(2,1)} %param.21) | copy-start | bytes 442372
  71.8 3.6 copy-start.1
  75.4 1.8 copy-start.18
  75.4 1.8 copy-start.20
  75.5 1.8 copy-start.11
  75.5 1.8 copy-start.27
  75.5 1.8 copy-start.31
  78.5 3.8 copy-start.22
  82.5 2.7 copy-start.17
  82.5 2.9 copy-start.14
  84.9 42.3 %reduce-scatter.24.cloned.1.call-start = ((), (), s32[]{:S(2)}) async-start(), calls=%async_computation.14 | async-start | bytes 184320
  86.8 2.9 copy-start.5
  88.4 62.4 %reduce-scatter.16.cloned.1.call-start = ((), (), s32[]{:S(2)}) async-start(), calls=%async_computation.10 | async-start | bytes 552960 | tf_op jit(solution)/shard_map/reduce_scatter | solution.py:273
  89.6 87.2 %reduce-scatter.18.cloned.1.call-start = ((), (), s32[]{:S(2)}) async-start(), calls=%async_computation.11 | async-start | bytes 921600 | tf_op jit(solution)/shard_map/reduce_scatter | solution.py:273
  90.9 1.8 copy-start.3
  90.9 1.8 copy-start.12
  90.9 1.8 copy-start.28
  90.9 112.1 %reduce-scatter.14.cloned.1.call-start = ((), (), s32[]{:S(2)}) async-start(), calls=%async_computation.9 | async-start | bytes 921600 | tf_op jit(solution)/shard_map/reduce_scatter | solution.py:273
  92.7 143.6 %reduce-scatter.22.cloned.1.call-start = ((), (), s32[]{:S(2)}) async-start(), calls=%async_computation.13 | async-start | bytes 2457600
  103.1 176.4 %reduce-scatter.20.cloned.1.call-start = ((), (), s32[]{:S(2)}) async-start(), calls=%async_computation.12 | async-start | bytes 4423680 | tf_op jit(solution)/shard_map/reduce_scatter | solution.py:273
  150.8 128.7 %copy-start.26 = (bf16[1,144,384]{2,1,0:T(8,128)(2,1)S(1)}, bf16[1,144,384]{2,1,0:T(8,128)(2,1)}, u32[]{:S(2)}) copy-start(bf16[1,144,384]{2,1,0:T(8,128)(2,1)} %reduce-scatter.16.cloned.1.call-done) | copy-start | bytes 331780
  176.8 102.7 %copy-start.24 = (bf16[1,144,576]{2,1,0:T(8,128)(2,1)S(1)}, bf16[1,144,576]{2,1,0:T(8,128)(2,1)}, u32[]{:S(2)}) copy-start(bf16[1,144,576]{2,1,0:T(8,128)(2,1)} %reduce-scatter.18.cloned.1.call-done) | copy-start | bytes 497668
  203.1 76.4 %copy-start.25 = (bf16[1,144,576]{2,1,0:T(8,128)(2,1)S(1)}, bf16[1,144,576]{2,1,0:T(8,128)(2,1)}, u32[]{:S(2)}) copy-start(bf16[1,144,576]{2,1,0:T(8,128)(2,1)} %reduce-scatter.14.cloned.1.call-done) | copy-start | bytes 497668
  (9 other events, 10.1 us)
Sparse Core Ops, SparseCore 0:
  9.6 39.8 all-gather.2
  51.0 20.7 all-gather.4
  85.0 19.6 reduce-scatter.25
  107.6 19.6 reduce-scatter.23
  129.6 21.1 reduce-scatter.15
  153.8 22.9 reduce-scatter.17
  180.1 22.9 reduce-scatter.13
  205.6 30.6 reduce-scatter.21
  239.0 40.4 reduce-scatter.19
where the time goes:
time: 434 us
  blocking collectives  187 us (43%)
  waiting for transfers between devices  172 us (40%)
  local copies, waits for them, and re-layouts  25.4 us (6%)
  matrix products  24.8 us (6%)
  between operations  15.8 us (4%)
  other arithmetic  7.81 us (2%)
    psum x1, blocking collectives, on_device(): stacked = lax.psum(shared, 'rep')  147 us
    reduce_scatter x4, waiting for transfers between devices, on_device(): lax.psum_scatter(shortened(stacked), 'fsdp', scatter_dimension=1, tiled=T...  116 us
    unnamed x12, waiting for transfers between devices  51.2 us
    unnamed x77, local copies, waits for them, and re-layouts  19.3 us
    all_gather x1, blocking collectives, on_device(): lax.all_gather(w_query, 'fsdp', axis=1, tiled=True)  12.8 us
    all_gather x1, blocking collectives, on_device(): lax.all_gather(w_keyval, 'fsdp', axis=1, tiled=True)  9.39 us
  transfers between devices with their start and end apart: 9, of which 7 were waited for; matrix products, arithmetic and copies ran while one was open for 10% of the time, Pallas kernels for 0%

commit v1 on v0

--- a/solution.py
+++ b/solution.py
@@ -10,6 +10,28 @@
 LEN = 64
 norm_eps = 1e-05
 rope_base = 100000.0
+
+
+def in_order(parts, dim):
+    parts = jnp.moveaxis(parts, 0, dim)
+    shape = parts.shape
+    return parts.reshape(*shape[:dim], shape[dim] * shape[dim + 1], *shape[dim + 2 :])
+
+
+def gather_around(shard, axis, dim):
+    size = lax.axis_size(axis)
+    pairs = [(i, (i + 1) % size) for i in range(size)]
+    back = [(b, a) for a, b in pairs]
+    lower, upper = ([], [])
+    for turn in range(size - 1):
+        if turn % 2 == 0:
+            lower.append(lax.ppermute(lower[-1] if lower else shard, axis, pairs))
+        else:
+            upper.append(lax.ppermute(upper[-1] if upper else shard, axis, back))
+    tiles = jnp.stack([*lower[::-1], shard, *upper])
+    shift = lax.axis_index(axis) - len(lower)
+    tiles = tiles[(jnp.arange(size) - shift) % size]
+    return in_order(tiles, dim)
 
 
 def shortened(value):
@@ -226,7 +248,7 @@
     live_rows = jnp.repeat(live_seqs, LEN)[:, None]
     gathered = (
         lax.all_gather(w_query, "fsdp", axis=1, tiled=True),
-        lax.all_gather(w_keyval, "fsdp", axis=1, tiled=True),
+        gather_around(w_keyval, "fsdp", 1),
         lax.all_gather(w_out, "fsdp", axis=1, tiled=True),
         lax.all_gather(w_gateup, "fsdp", axis=1, tiled=True),
         lax.all_gather(w_down, "fsdp", axis=1, tiled=True),

time: 434 us -> 436 us (level)
    unnamed x77 -> x87, local copies, waits for them, and re-layouts: 19.3 us -> 18.4 us
  transfers between devices with their start and end apart: 9 -> 12, of which waited for: 7 -> 8; matrix products, arithmetic and copies ran while one was open for 10% -> 8% of each run, Pallas kernels for 0% -> 0%
where the time goes in v1:
time: 436 us
  blocking collectives  184 us (42%)
  waiting for transfers between devices  176 us (40%)
  local copies, waits for them, and re-layouts  25.3 us (6%)
  matrix products  24.6 us (6%)
  between operations  15.9 us (4%)
  other arithmetic  6.25 us (1%)
    psum x1, blocking collectives, on_device(): stacked = lax.psum(shared, 'rep')  147 us
    reduce_scatter x4, waiting for transfers between devices, on_device(): lax.psum_scatter(shortened(stacked), 'fsdp', scatter_dimension=1, tiled=T...  116 us
    unnamed x12, waiting for transfers between devices  53.1 us
    unnamed x87, local copies, waits for them, and re-layouts  18.4 us
    all_gather x1, blocking collectives, on_device(): lax.all_gather(w_query, 'fsdp', axis=1, tiled=True)  12.5 us
  transfers between devices with their start and end apart: 12, of which 8 were waited for; matrix products, arithmetic and copies ran while one was open for 8% of the time, Pallas kernels for 0%

profile of v1, /device:TPU:0, one launch (start us, length us, event | category | flops | bytes accessed | tf_op | source)
XLA Modules:
  0.0 435.8 jit_solution(821116877132136870)
XLA Ops:
  8.0 2.4 collective-permute-start.2
  10.6 8.6 %all_gather.33 = bf16[1,576,384]{2,1,0:T(8,128)(2,1)} all-gather(bf16[1,144,384]{2,1,0:T(8,128)(2,1)} %param.15), channel_id=1, replica_groups=mesh['rep'=8,'fsdp'=4] {'fsdp'}, dimensions={1}, use_global_device_ids=true | all-gather | bytes 552960 | tf_op jit(solution)/shard_map/all_gather | solution.py:268
  20.9 7.2 %all-reduce.3 = (bf16[576]{0:T(1024)(128)(2,1)S(1)}, bf16[576]{0:T(1024)(128)(2,1)S(1)}) all-reduce(bf16[576]{0:T(1024)(128)(2,1)S(1)} %dynamic-update-slice, bf16[576]{0:T(1024)(128)(2,1)S(1)} %dynamic-update-slice.1), channel_id=1, replica_groups=mesh['rep'=8,'fsdp'=4] {'fsdp'}, use_global_device_ids=true, to_apply=%add | all-reduce | flops 1152 | bytes 4608
  28.7 12.5 %all_gather.28 = bf16[1,576,576]{2,1,0:T(8,128)(2,1)S(1)} all-gather(bf16[1,144,576]{2,1,0:T(8,128)(2,1)S(1)} %copy-done.22), channel_id=1, replica_groups=mesh['rep'=8,'fsdp'=4] {'fsdp'}, dimensions={1}, use_global_device_ids=true | all-gather | bytes 829440 | tf_op jit(solution)/shard_map/all_gather | solution.py:250
  42.5 1.1 fusion.65
  43.6 8.5 %all_gather.29 = bf16[1,576,576]{2,1,0:T(8,128)(2,1)S(1)} all-gather(bf16[1,144,576]{2,1,0:T(8,128)(2,1)S(1)} %copy-done.23), channel_id=1, replica_groups=mesh['rep'=8,'fsdp'=4] {'fsdp'}, dimensions={1}, use_global_device_ids=true | all-gather | bytes 829440 | tf_op jit(solution)/shard_map/all_gather | solution.py:252
  53.6 3.8 collective-permute-done.1
  62.3 4.1 fusion.3
  66.4 3.2 all-gather.5.cloned.1.call-done
  69.6 3.6 multiply_convert_fusion.1
  73.3 1.8 multiply_reduce_fusion.1
  75.2 1.0 convolution_convert_fusion.6
  76.2 1.1 reshape.283
  77.3 1.2 multiply_reduce_fusion
  78.5 0.9 fusion.26
  83.7 0.9 broadcast_multiply_fusion.1
  84.7 0.9 fusion.58
  88.2 1.1 fusion.15
  89.8 1.3 fusion.10
  91.2 1.2 fusion.11
  93.1 6.0 %copy.98 = bf16[1,1536,576]{2,0,1:T(2,128)(2,1)} copy(bf16[1,1536,576]{1,2,0:T(8,128)(2,1)S(1)} %fusion.5) | data formatting | bytes 3538944
  99.1 3.7 copy.124
  103.9 2.9 fusion
  108.3 1.3 fusion.20
  110.5 19.0 %reduce-scatter.26.cloned.1.call-done = bf16[144,1]{1,0:T(8,128)(2,1)} async-done(((bf16[576,1]{1,0:T(8,128)(2,1)}), bf16[144,1]{1,0:T(8,128)(2,1)}) %reduce-scatter.26.cloned.1.call-update) | async-done | bytes 304
  130.4 22.7 %reduce-scatter.16.cloned.1.call-done = bf16[1,144,384]{2,1,0:T(8,128)(2,1)} async-done(((bf16[1,576,384]{2,1,0:T(8,128)(2,1)}), bf16[1,144,384]{2,1,0:T(8,128)(2,1)}) %reduce-scatter.16.cloned.1.call-update) | async-done | bytes 110608 | tf_op jit(solution)/shard_map/reduce_scatter | solution.py:295
  153.1 26.0 %reduce-scatter.14.cloned.1.call-done = bf16[1,144,576]{2,1,0:T(8,128)(2,1)} async-done(((bf16[1,576,576]{2,1,0:T(8,128)(2,1)}), bf16[1,144,576]{2,1,0:T(8,128)(2,1)}) %reduce-scatter.14.cloned.1.call-update) | async-done | bytes 165904 | tf_op jit(solution)/shard_map/reduce_scatter | solution.py:295
  179.1 26.3 %reduce-scatter.18.cloned.1.call-done = bf16[1,144,576]{2,1,0:T(8,128)(2,1)} async-done(((bf16[1,576,576]{2,1,0:T(8,128)(2,1)}), bf16[1,144,576]{2,1,0:T(8,128)(2,1)}) %reduce-scatter.18.cloned.1.call-update) | async-done | bytes 165904 | tf_op jit(solution)/shard_map/reduce_scatter | solution.py:295
  205.4 33.2 %reduce-scatter.22.cloned.1.call-done = bf16[384,576]{1,0:T(8,128)(2,1)} async-done(((bf16[1536,576]{1,0:T(8,128)(2,1)}), bf16[384,576]{1,0:T(8,128)(2,1)}) %reduce-scatter.22.cloned.1.call-update) | async-done | bytes 442384
  238.6 1.5 reshape_bitcast_fusion
  240.8 41.0 %reduce-scatter.20.cloned.1.call-done = bf16[1,144,3072]{2,1,0:T(8,128)(2,1)} async-done(((bf16[1,576,3072]{2,1,0:T(8,128)(2,1)}), bf16[1,144,3072]{2,1,0:T(8,128)(2,1)}) %reduce-scatter.20.cloned.1.call-update) | async-done | bytes 884752 | tf_op jit(solution)/shard_map/reduce_scatter | solution.py:295
  281.8 147.5 %all-reduce.5 = (f32[1,144,576]{2,1,0:T(8,128)}, f32[1,144,384]{2,1,0:T(8,128)}, f32[1,144,576]{2,1,0:T(8,128)}, f32[1,144,3072]{2,1,0:T(8,128)}, f32[1,384,576]...) all-reduce(bf16[1,144,576]{2,1,0:T(8,128)(2,1)S(1)} %copy-done.24, ...), channel_id=1, replica_groups=mesh['rep'=8,'fsdp'=4] {'rep'}, use_global_device_ids=true, to_apply=%region_8.9 | all-reduce | flops 885024 | bytes 5310144 | tf_op jit(solution)/shard_map/psum | solution.py:297
  (177 shorter events, 22.5 us)
Async XLA Ops:
  7.2 12.0 %copy-start.36 = (u32[32]{0:T(128)S(1)}, u32[32]{0:T(128)}, u32[]{:S(2)}) copy-start(u32[32]{0:T(128)} %constant.56) | copy-start | bytes 388
  7.2 11.9 %copy-start.31 = (bf16[1,144]{1,0:T(2,128)(2,1)S(1)}, bf16[1,144]{1,0:T(2,128)(2,1)}, u32[]{:S(2)}) copy-start(bf16[1,144]{1,0:T(2,128)(2,1)} %param.19) | copy-start | bytes 868
  7.2 12.0 %copy-start.32 = (bf16[1,144]{1,0:T(2,128)(2,1)S(1)}, bf16[1,144]{1,0:T(2,128)(2,1)}, u32[]{:S(2)}) copy-start(bf16[1,144]{1,0:T(2,128)(2,1)} %param.20) | copy-start | bytes 868
  7.2 20.9 %copy-start = (bf16[128,576]{0,1:T(8,128)(2,1)S(1)}, bf16[128,576]{0,1:T(8,128)(2,1)}, u32[]{:S(2)}) copy-start(bf16[128,576]{0,1:T(8,128)(2,1)} %param.11) | copy-start | bytes 442372
  7.2 21.5 %copy-start.22 = (bf16[1,144,576]{2,1,0:T(8,128)(2,1)S(1)}, bf16[1,144,576]{2,1,0:T(8,128)(2,1)}, u32[]{:S(2)}) copy-start(bf16[1,144,576]{2,1,0:T(8,128)(2,1)} %param.14) | copy-start | bytes 497668
  7.2 55.1 %all-gather.3.cloned.1.call-start = ((), (), s32[]{:S(2)}) async-start(), calls=%async_computation.7 | async-start | bytes 4423680 | tf_op jit(solution)/shard_map/all_gather | solution.py:253
  8.0 61.7 %all-gather.5.cloned.1.call-start = ((), (), s32[]{:S(2)}) async-start(), calls=%async_computation.8 | async-start | bytes 2211840 | tf_op jit(solution)/shard_map/all_gather | solution.py:254
  8.0 45.6 %collective-permute-start.2 = (bf16[1,144,384]{2,1,0:T(8,128)(2,1)}, bf16[1,144,384]{2,1,0:T(8,128)(2,1)S(1)}, u32[]{:S(2)}, u32[]{:S(2)}) collective-permute-start(bf16[1,144,384]{2,1,0:T(8,128)(2,1)} %param.15), channel_id=1, source_target_pairs={{1,0},{2,1},{3,2},{0,3},{5,4},{6,5},{7,6},{4,7},{9,8},{10,9},{11,1... | collective-permute-start | bytes 331784 | tf_op jit(solution)/shard_map/ppermute | solution.py:30
  10.4 42.6 %collective-permute-start = (bf16[1,144,384]{2,1,0:T(8,128)(2,1)}, bf16[1,144,384]{2,1,0:T(8,128)(2,1)S(1)}, u32[]{:S(2)}, u32[]{:S(2)}) collective-permute-start(bf16[1,144,384]{2,1,0:T(8,128)(2,1)} %param.15), channel_id=1, source_target_pairs={{0,1},{1,2},{2,3},{3,0},{4,5},{5,6},{6,7},{7,4},{8,9},{9,10},{10,1... | collective-permute-start | bytes 331784 | tf_op jit(solution)/shard_map/ppermute | solution.py:28
  10.5 99.2 %reduce-scatter.24.cloned.1.call-start = ((), (), s32[]{:S(2)}) async-start(), calls=%async_computation.14 | async-start | bytes 184320
  42.1 15.3 %copy-start.14 = (bf16[1,144,384]{2,1,0:T(8,128)(2,1)S(1)}, bf16[1,144,384]{2,1,0:T(8,128)(2,1)}, u32[]{:S(2)}) copy-start(bf16[1,144,384]{2,1,0:T(8,128)(2,1)} %param.15) | copy-start | bytes 331780
  42.4 15.0 %copy-start.7 = (f32[128,64]{0,1:T(8,128)}, f32[128,64]{0,1:T(8,128)S(1)}, u32[]{:S(2)}) copy-start(f32[128,64]{0,1:T(8,128)S(1)} %get-tuple-element.37) | copy-start | bytes 98308
  42.4 15.8 %copy-start.12 = (f32[128,64]{0,1:T(8,128)}, f32[128,64]{0,1:T(8,128)S(1)}, u32[]{:S(2)}) copy-start(f32[128,64]{0,1:T(8,128)S(1)} %get-tuple-element.38) | copy-start | bytes 98308
  53.1 16.5 %copy-start.27 = (f32[128]{0:T(128)}, f32[128]{0:T(128)S(1)}, u32[]{:S(2)}) copy-start(f32[128]{0:T(128)S(1)} %mul.340) | copy-start | bytes 1540
  53.1 4.3 collective-permute-start.1
  62.3 7.3 %copy-start.10 = (bf16[128,576]{0,1:T(8,128)(2,1)S(1)}, bf16[128,576]{0,1:T(8,128)(2,1)}, u32[]{:S(2)}) copy-start(bf16[128,576]{0,1:T(8,128)(2,1)} %param.21) | copy-start | bytes 442372
  69.6 3.6 copy-start.1
  79.8 2.8 copy-start.13
  82.7 2.9 copy-start.3
  83.5 3.8 copy-start.30
  85.6 4.1 copy-start.9
  87.3 42.3 %reduce-scatter.26.cloned.1.call-start = ((), (), s32[]{:S(2)}) async-start(), calls=%async_computation.15 | async-start | bytes 184320
  88.2 64.9 %reduce-scatter.16.cloned.1.call-start = ((), (), s32[]{:S(2)}) async-start(), calls=%async_computation.10 | async-start | bytes 552960 | tf_op jit(solution)/shard_map/reduce_scatter | solution.py:295
  89.3 89.7 %reduce-scatter.14.cloned.1.call-start = ((), (), s32[]{:S(2)}) async-start(), calls=%async_computation.9 | async-start | bytes 921600 | tf_op jit(solution)/shard_map/reduce_scatter | solution.py:295
  89.8 2.7 copy-start.4
  89.8 2.7 copy-start.11
  91.1 114.3 %reduce-scatter.18.cloned.1.call-start = ((), (), s32[]{:S(2)}) async-start(), calls=%async_computation.11 | async-start | bytes 921600 | tf_op jit(solution)/shard_map/reduce_scatter | solution.py:295
  92.4 146.2 %reduce-scatter.22.cloned.1.call-start = ((), (), s32[]{:S(2)}) async-start(), calls=%async_computation.13 | async-start | bytes 2457600
  102.8 179.0 %reduce-scatter.20.cloned.1.call-start = ((), (), s32[]{:S(2)}) async-start(), calls=%async_computation.12 | async-start | bytes 4423680 | tf_op jit(solution)/shard_map/reduce_scatter | solution.py:295
  153.1 128.7 %copy-start.26 = (bf16[1,144,384]{2,1,0:T(8,128)(2,1)S(1)}, bf16[1,144,384]{2,1,0:T(8,128)(2,1)}, u32[]{:S(2)}) copy-start(bf16[1,144,384]{2,1,0:T(8,128)(2,1)} %reduce-scatter.16.cloned.1.call-done) | copy-start | bytes 331780
  179.1 102.7 %copy-start.24 = (bf16[1,144,576]{2,1,0:T(8,128)(2,1)S(1)}, bf16[1,144,576]{2,1,0:T(8,128)(2,1)}, u32[]{:S(2)}) copy-start(bf16[1,144,576]{2,1,0:T(8,128)(2,1)} %reduce-scatter.14.cloned.1.call-done) | copy-start | bytes 497668
  205.4 76.4 %copy-start.25 = (bf16[1,144,576]{2,1,0:T(8,128)(2,1)S(1)}, bf16[1,144,576]{2,1,0:T(8,128)(2,1)}, u32[]{:S(2)}) copy-start(bf16[1,144,576]{2,1,0:T(8,128)(2,1)} %reduce-scatter.18.cloned.1.call-done) | copy-start | bytes 497668
  (17 other events, 25.5 us)
Sparse Core Ops, SparseCore 0:
  9.6 37.5 all-gather.2
  48.8 20.8 all-gather.4
  87.4 19.6 reduce-scatter.23
  109.9 19.6 reduce-scatter.25
  131.9 21.1 reduce-scatter.15
  156.1 22.9 reduce-scatter.13
  182.4 22.9 reduce-scatter.17
  208.0 30.6 reduce-scatter.21
  241.3 40.4 reduce-scatter.19
